TPU v7x, 32 devices: a whole 2x2x4 slice. The times are simulated.
32 devices in a mesh: groups: 2 (over y), dom: 4 (over z), sub: 4 (over x, core).
Axes of the slice: x: 2, y: 2, z: 4, core: 2. Of those that a mesh axis runs over, the one named last changes fastest.
Arguments:
- positions: float32 [3, 16, 16, 128], P(None, ('groups', 'dom'), 'sub'), parts along dimension 1, may hold values from -50 to 80, as said below
- charge: float32 [16, 16, 128], P(('groups', 'dom'), 'sub'), parts along dimension 0, may hold values from -2.5 to 2.5
- radius: float32 [16, 16, 128], P(('groups', 'dom'), 'sub'), parts along dimension 0, may hold values from 1.3 to 2.2
- segment: int32 [16, 16, 128], P(('groups', 'dom'), 'sub'), parts along dimension 0, may hold values from 0 to 15, never falling along the last dimension, each value on 1 to 16 neighbouring positions
- near_tiles: int32 [16, 16, 8], P(('groups', 'dom'), 'sub'), parts along dimension 0, may hold values from 0 to 1, as said below
Outputs:
- born_radii: float32 [16, 16, 128], P(('groups', 'dom'), 'sub'), parts along dimension 0
- radius_grad: float32 [16, 16, 128], P(('groups', 'dom'), 'sub'), parts along dimension 0
- forces: float32 [3, 16, 16, 128], P(None, ('groups', 'dom'), 'sub'), parts along dimension 1
There are 2 independent parts, one for each index of `groups`. A program takes and returns all parts, laid end to end along the dimension named above; each array names one. Nothing has to cross between parts.
Inputs may be any that keep to these rules, and one draw needn't show every extreme that they name: `positions`: coordinates in angstroms; the third runs along the fiber. near_tiles[a, b, k] is 1 when the partner tile of step k is near tile (a, b), else 0. The relation is symmetric: a tile is near its partner exactly when the partner is near it by the opposite step. No tile is near a tile beyond either end of the first tile dimension; the second dimension closes around the fiber. `segment`: within each tile the component numbers never fall along the atoms, and each of the 16 components has 1 to 16 atoms.
All inputs are finite; a program needn't handle non-finite values.
Results may differ from a plain program's by a relative error of at most 0.0003.
Values sent between devices are 32-bit elements; how exact they have to be, the bound alone decides.
No kernel may reach another device: no remote copies, remote signals or barrier semaphores. Data moves between devices by JAX's collectives and lax.ppermute only.
A program may use at most 64 MiB of HBM per device.

v0:
```python
import jax
import jax.numpy as jnp
from jax import lax
from jax.sharding import PartitionSpec as P

CT = 16
neighbour_steps = ((-1, -1), (-1, 0), (-1, 1), (0, -1), (0, 1), (1, -1), (1, 0), (1, 1))
switch_span = 64.0
radius_factor = 1.5
highest = lax.Precision.HIGHEST
far_block = 1024


def passed_along(shard, axis, by):
    size = lax.axis_size(axis)
    return lax.ppermute(shard, axis, [(i, (i + by) % size) for i in range(size)])


def extended(cells, sides, width):
    for axis, dim in sides:
        count = lax.axis_size(axis)
        head = lax.slice_in_dim(cells, 0, width, axis=dim)
        tail = lax.slice_in_dim(cells, cells.shape[dim] - width, cells.shape[dim], axis=dim)
        cells = jnp.concatenate(
            [
                lax.ppermute(tail, axis, [(i, (i + 1) % count) for i in range(count)]),
                cells,
                lax.ppermute(head, axis, [((i + 1) % count, i) for i in range(count)]),
            ],
            axis=dim,
        )
    return cells


def far_keep(tile_along, tile_round, tile_near, comp_along, comp_round, around_count):
    struck = (tile_along[:, None] == comp_along[None, :]) & (
        tile_round[:, None] == comp_round[None, :]
    )
    for slot_index, (step_z, step_s) in enumerate(neighbour_steps):
        flagged = (tile_near[:, slot_index] == 1)[:, None]
        same_along = (tile_along + step_z)[:, None] == comp_along[None, :]
        same_round = jnp.mod(tile_round + step_s, around_count)[:, None] == comp_round[None, :]
        struck = struck | flagged & same_along & same_round
    return jnp.logical_not(struck)


def pair_distance(own_pos, part_pos):
    dist_sq = jnp.zeros(own_pos.shape[1:] + (part_pos.shape[-1],), own_pos.dtype)
    for axis_slot in range(3):
        apart_axis = own_pos[axis_slot][..., :, None] - part_pos[axis_slot][..., None, :]
        dist_sq = dist_sq + apart_axis * apart_axis
    return dist_sq


def born_distance(dist_sq, product):
    return jnp.sqrt(dist_sq + product * jnp.exp(-dist_sq / (4.0 * product)))


def tile_screen(own_pos, part_pos, part_rho, keep_mask):
    dist_sq = pair_distance(own_pos, part_pos)
    radius_sq = part_rho[..., None, :] * part_rho[..., None, :]
    denom_sq = dist_sq + radius_sq
    pair_term = radius_sq * part_rho[..., None, :] / (denom_sq * denom_sq)
    return jnp.sum(jnp.where(keep_mask, pair_term, 0.0), axis=-1)


def tile_energy(own_pos, own_born, part_pos, part_q, part_born, keep_mask):
    dist_sq = pair_distance(own_pos, part_pos)
    product = own_born[..., :, None] * part_born[..., None, :]
    pair_term = part_q[..., None, :] / born_distance(dist_sq, product)
    return jnp.sum(jnp.where(keep_mask, pair_term, 0.0), axis=-1)


def centre_distance(flat_pos, centre):
    dist_sq = jnp.zeros((flat_pos.shape[1], centre.shape[1]), flat_pos.dtype)
    for axis_slot in range(3):
        apart_axis = flat_pos[axis_slot][:, None] - centre[axis_slot][None, :]
        dist_sq = dist_sq + apart_axis * apart_axis
    return dist_sq


def screen_block(flat_pos, centre, volume, comp_radius, keep):
    dist_sq = centre_distance(flat_pos, centre)
    weight = dist_sq / (dist_sq + switch_span)
    denom_sq = dist_sq + comp_radius * comp_radius
    return jnp.sum(jnp.where(keep, volume * weight / (denom_sq * denom_sq), 0.0), axis=1)


def potential_block(flat_pos, flat_born, centre, total_q, comp_radius, keep):
    dist_sq = centre_distance(flat_pos, centre)
    weight = dist_sq / (dist_sq + switch_span)
    product = flat_born[:, None] * comp_radius[None, :]
    return jnp.sum(jnp.where(keep, total_q * weight / born_distance(dist_sq, product), 0.0), axis=1)


def block_split(values, block_size):
    shaped = values.reshape(values.shape[:-1] + (values.shape[-1] // block_size, block_size))
    return jnp.moveaxis(shaped, -2, 0)


def far_screening(flat_pos, centre, volume, comp_radius, comp_along, comp_round, keep_fn):
    block_size = min(centre.shape[1], far_block)

    def accumulate(running, pieces):
        keep = keep_fn(pieces[3], pieces[4])
        return (running + screen_block(flat_pos, pieces[0], pieces[1], pieces[2], keep), None)

    inputs = (
        block_split(centre, block_size),
        block_split(volume, block_size),
        block_split(comp_radius, block_size),
        block_split(comp_along, block_size),
        block_split(comp_round, block_size),
    )
    return lax.scan(
        jax.checkpoint(accumulate), jnp.zeros((flat_pos.shape[1],), jnp.float32), inputs
    )[0]


def far_potential(
    flat_pos, flat_born, centre, total_q, comp_radius, comp_along, comp_round, keep_fn
):
    block_size = min(centre.shape[1], far_block)

    def accumulate(running, pieces):
        keep = keep_fn(pieces[3], pieces[4])
        return (
            running + potential_block(flat_pos, flat_born, pieces[0], pieces[1], pieces[2], keep),
            None,
        )

    inputs = (
        block_split(centre, block_size),
        block_split(total_q, block_size),
        block_split(comp_radius, block_size),
        block_split(comp_along, block_size),
        block_split(comp_round, block_size),
    )
    return lax.scan(
        jax.checkpoint(accumulate), jnp.zeros((flat_pos.shape[1],), jnp.float32), inputs
    )[0]


def components(positions, charge, radius, segment):
    onehot = (segment[..., None] == jnp.arange(CT, dtype=jnp.int32)).astype(jnp.float32)
    members = jnp.sum(onehot, axis=2)
    centre = jnp.einsum("kabl,ablc->kabc", positions, onehot, precision=highest) / members
    total_q = jnp.einsum("abl,ablc->abc", charge, onehot, precision=highest)
    volume = jnp.einsum("abl,ablc->abc", radius * radius * radius, onehot, precision=highest)
    comp_radius = (
        radius_factor * jnp.einsum("abl,ablc->abc", radius, onehot, precision=highest) / members
    )
    return (onehot, members, centre, total_q, volume, comp_radius)


def sub_pass(rim_piece, direction):
    return passed_along(rim_piece, "sub", direction)


def dom_pass(rim_piece, direction):
    return passed_along(rim_piece, "dom", direction)


def fold_rims(window_grad):
    tile_rows = window_grad.shape[1] - 2
    tile_cols = window_grad.shape[2] - 2
    inner_grid = window_grad[:, :, 1 : tile_cols + 1]
    inner_grid = inner_grid.at[:, :, tile_cols - 1].add(sub_pass(window_grad[:, :, 0], -1))
    inner_grid = inner_grid.at[:, :, 0].add(sub_pass(window_grad[:, :, tile_cols + 1], 1))
    own_grid = inner_grid[:, 1 : tile_rows + 1]
    own_grid = own_grid.at[:, tile_rows - 1].add(dom_pass(inner_grid[:, 0], -1))
    own_grid = own_grid.at[:, 0].add(dom_pass(inner_grid[:, tile_rows + 1], 1))
    return own_grid


def centre_spread(grad_table):
    partial_sums = lax.psum_scatter(grad_table, "dom", scatter_dimension=1, tiled=True)
    return lax.psum_scatter(partial_sums, "sub", scatter_dimension=1, tiled=True)


def local(positions, charge, radius, segment, near_tiles):
    tile_rows, tile_cols, tile_width = charge.shape
    sub_count = lax.axis_size("sub")
    around_count = tile_cols * sub_count
    self_keep = jnp.arange(tile_width)[:, None] != jnp.arange(tile_width)[None, :]
    atom_stack = jnp.concatenate([positions, charge[None], radius[None]], axis=0)
    window = extended(atom_stack, (("dom", 1), ("sub", 2)), 1)
    win_pos = window[0:3]
    win_q = window[3]
    win_rho = window[4]
    onehot, members, centre, total_q, volume, comp_radius = components(
        positions, charge, radius, segment
    )
    comp_table = jnp.concatenate(
        [
            centre.reshape(3, -1),
            total_q.reshape(1, -1),
            volume.reshape(1, -1),
            comp_radius.reshape(1, -1),
        ],
        axis=0,
    )
    sub_table = lax.all_gather(comp_table, "sub", axis=1, tiled=True)
    all_table = lax.all_gather(sub_table, "dom", axis=1, tiled=True)
    all_centre = all_table[0:3]
    all_charge = all_table[3]
    all_volume = all_table[4]
    all_radius = all_table[5]
    per_device = tile_rows * tile_cols * CT
    entry_index = jnp.arange(all_table.shape[1], dtype=jnp.int32)
    owner_device = entry_index // per_device
    local_entry = entry_index % per_device
    comp_along = owner_device // sub_count * tile_rows + local_entry // (tile_cols * CT)
    comp_round = owner_device % sub_count * tile_cols + local_entry // CT % tile_cols
    dom_index = lax.axis_index("dom")
    sub_index = lax.axis_index("sub")
    shape_three = (tile_rows, tile_cols, tile_width)
    along_grid = dom_index * tile_rows + jnp.arange(tile_rows, dtype=jnp.int32)[:, None, None]
    round_grid = sub_index * tile_cols + jnp.arange(tile_cols, dtype=jnp.int32)[None, :, None]
    tile_along = jnp.broadcast_to(along_grid, shape_three).reshape(-1)
    tile_round = jnp.broadcast_to(round_grid, shape_three).reshape(-1)
    tile_near = jnp.broadcast_to(near_tiles[:, :, None, :], shape_three + (8,)).reshape(-1, 8)

    def keep_fn(block_along, block_round):
        return far_keep(tile_along, tile_round, tile_near, block_along, block_round, around_count)

    def window_part(values, step_z, step_s):
        return values[
            ..., 1 + step_z : 1 + step_z + tile_rows, 1 + step_s : 1 + step_s + tile_cols, :
        ]

    def born_of(own_pos, near_pos, far_centre):
        screening = tile_screen(
            own_pos, window_part(near_pos, 0, 0), window_part(win_rho, 0, 0), self_keep
        )
        for slot_index, (step_z, step_s) in enumerate(neighbour_steps):
            keep_mask = (near_tiles[..., slot_index] == 1)[..., None, None]
            screening = screening + tile_screen(
                own_pos,
                window_part(near_pos, step_z, step_s),
                window_part(win_rho, step_z, step_s),
                keep_mask,
            )
        far_part = far_screening(
            own_pos.reshape(3, -1),
            far_centre,
            all_volume,
            all_radius,
            comp_along,
            comp_round,
            keep_fn,
        )
        screening = screening + far_part.reshape(screening.shape)
        return radius * (1.0 + radius * screening)

    born_radii, born_back = jax.vjp(born_of, positions, win_pos, all_centre)
    win_born = extended(born_radii, (("dom", 0), ("sub", 1)), 1)

    def energy_of(own_pos, own_born, near_pos, near_born, far_centre):
        potential = tile_energy(
            own_pos,
            own_born,
            window_part(near_pos, 0, 0),
            window_part(win_q, 0, 0),
            window_part(near_born, 0, 0),
            self_keep,
        )
        for slot_index, (step_z, step_s) in enumerate(neighbour_steps):
            keep_mask = (near_tiles[..., slot_index] == 1)[..., None, None]
            potential = potential + tile_energy(
                own_pos,
                own_born,
                window_part(near_pos, step_z, step_s),
                window_part(win_q, step_z, step_s),
                window_part(near_born, step_z, step_s),
                keep_mask,
            )
        far_part = far_potential(
            own_pos.reshape(3, -1),
            own_born.reshape(-1),
            far_centre,
            all_charge,
            all_radius,
            comp_along,
            comp_round,
            keep_fn,
        )
        potential = potential + far_part.reshape(potential.shape)
        return -0.5 * jnp.sum(charge * (charge / own_born + potential))

    energy_back = jax.vjp(energy_of, positions, born_radii, win_pos, win_born, all_centre)[1]
    grad_pos, grad_born, grad_window, grad_wborn, grad_centre = energy_back(
        jnp.ones((), jnp.float32)
    )
    radius_grad = grad_born + fold_rims(grad_wborn[None])[0]
    chain_pos, chain_window, chain_centre = born_back(radius_grad)
    own_centre = centre_spread(grad_centre + chain_centre)
    per_member = own_centre.reshape(centre.shape) / members
    centre_part = jnp.einsum("ablc,kabc->kabl", onehot, per_member, precision=highest)
    total_grad = grad_pos + chain_pos + fold_rims(grad_window + chain_window) + centre_part
    return (born_radii, radius_grad, -total_grad)


def solution(mesh):
    placed = (
        P(None, ("groups", "dom"), "sub", None),
        P(("groups", "dom"), "sub", None),
        P(("groups", "dom"), "sub", None),
        P(("groups", "dom"), "sub", None),
        P(("groups", "dom"), "sub", None),
    )
    return jax.shard_map(
        local,
        mesh=mesh,
        in_specs=placed,
        out_specs=(
            P(("groups", "dom"), "sub", None),
            P(("groups", "dom"), "sub", None),
            P(None, ("groups", "dom"), "sub", None),
        ),
        check_vma=False,
    )
```

profile of v0, /device:TPU:0, one launch (start us, length us, event | category | flops | bytes accessed | tf_op | source)
XLA Modules:
  0.0 267.3 jit_solution(454773463730050776)
XLA Ops:
  8.0 3.1 %collective-permute-start = (f32[5,1,4,128]{3,2,1,0:T(4,128)S(1)}, f32[5,1,4,128]{3,2,1,0:T(4,128)S(1)}, u32[]{:S(2)}, u32[]{:S(2)}) collective-permute-start(f32[5,1,4,128]{3,2,1,0:T(4,128)S(1)} %get-tuple-element.1764), channel_id=1, source_target_pairs={{0,4},{4,8},{8,12},{12,0},{1,5},{5,9},{9,13},{13,1},{2,6},{6,10},{... | collective-permute-start | bytes 30728 | tf_op jit(solution)/shard_map/ppermute | solution.py:26
  11.1 2.1 collective-permute-start.1
  20.8 5.2 %all_gather.6 = f32[6,512]{1,0:T(8,128)S(1)} all-gather(f32[6,128]{1,0:T(8,128)S(1)} %pad_maximum_fusion.40), channel_id=1, replica_groups=mesh['groups'=2,'dom'=4,'sub'=4] {'sub'}, dimensions={1}, use_global_device_ids=true | all-gather | bytes 15360 | tf_op jit(solution)/shard_map/all_gather | solution.py:203
  26.8 13.1 %all_gather.7 = f32[6,2048]{1,0:T(8,128)S(1)} all-gather(f32[6,512]{1,0:T(8,128)S(1)} %all_gather.6), channel_id=1, replica_groups=mesh['groups'=2,'dom'=4,'sub'=4] {'dom'}, dimensions={1}, use_global_device_ids=true | all-gather | bytes 61440 | tf_op jit(solution)/shard_map/all_gather | solution.py:204
  44.9 20.9 %while.65 = (s32[]{:T(128)}, f32[1024]{0:T(1024)S(1)}, s32[2,1024]{1,0:T(2,128)S(1)}, s32[2,1024]{1,0:T(2,128)S(1)}, pred[1024,1]{0,1:T(4,128)(4,1)S(1)}, /*inde...) while((s32[]{:T(128)}, f32[1024]{0:T(1024)S(1)}, ...), condition=%wide.region_12.13_spmd.clone.clone.clone, body=%wide.region_10.12_spmd.clone.clone.clone.sunk | while | flops 50371588 | bytes 205115 | solution.py:115
  45.4 10.0 %select_reduce_fusion.11 = f32[1024]{0:T(1024)S(1)} fusion(f32[1024]{0:T(1024)S(1)} %bitcast.622, f32[1024]{0:T(1024)S(1)} %bitcast.592, f32[1024]{0:T(1024)S(1)} %bitcast.691, f32[1024]{0:T(1024)S(1)} %bitcast.591, f32[1024]{0:T(1024)S(1)} %bitcast.695, f32[1024]{0:T(1024)S(1)} %bitcast.590, f32[1024]{0:T(1024)S(1)} %bitcast.693, ...), kind=kLoop, calls=%fused_computation.229.clone.1 | loop fusion | flops 50330624 | bytes 81920 | tf_op jit(solution)/shard_map/jvp()/while/body/eval_jaxpr/reduce_sum | solution.py:86
  55.8 10.0 %select_reduce_fusion.11 = f32[1024]{0:T(1024)S(1)} fusion(f32[1024]{0:T(1024)S(1)} %bitcast.622, f32[1024]{0:T(1024)S(1)} %bitcast.592, f32[1024]{0:T(1024)S(1)} %bitcast.691, f32[1024]{0:T(1024)S(1)} %bitcast.591, f32[1024]{0:T(1024)S(1)} %bitcast.695, f32[1024]{0:T(1024)S(1)} %bitcast.590, f32[1024]{0:T(1024)S(1)} %bitcast.693, ...), kind=kLoop, calls=%fused_computation.229.clone.1 | loop fusion | flops 50330624 | bytes 81920 | tf_op jit(solution)/shard_map/jvp()/while/body/eval_jaxpr/reduce_sum | solution.py:86
  70.1 3.7 %collective-permute-start.5 = (f32[1,4,128]{2,1,0:T(4,128)S(1)}, f32[1,4,128]{2,1,0:T(4,128)S(1)}, u32[]{:S(2)}, u32[]{:S(2)}) collective-permute-start(f32[1,4,128]{2,1,0:T(4,128)S(1)} %get-tuple-element.1814), channel_id=1, source_target_pairs={{4,0},{8,4},{12,8},{0,12},{5,1},{9,5},{13,9},{1,13},{6,2},{10,6},{... | collective-permute-start | bytes 6152 | tf_op jit(solution)/shard_map/ppermute | solution.py:28
  73.8 61.9 %while.63 = (s32[]{:T(128)}, f32[3,1024]{1,0:T(4,128)S(1)}, f32[1024]{0:T(1024)S(1)}, f32[1024]{0:T(1024)S(1)}, f32[2,3,1024]{2,1,0:T(4,128)S(1)}, /*index=5*/f3...) while((s32[]{:T(128)}, f32[3,1024]{1,0:T(4,128)S(1)}, ...), condition=%wide.region_21.22_spmd.clone, body=%wide.region_13.21_spmd.clone.sunk | while | flops 160494592 | bytes 520676 | solution.py:139
  74.3 14.4 %multiply_reduce_fusion.20 = f32[1024]{0:T(1024)S(1)} fusion(f32[1024]{0:T(1024)S(1)} %bitcast.599, f32[1024]{0:T(1024)S(1)} %get-tuple-element.2180, f32[1024]{0:T(1024)S(1)} %bitcast.606, f32[1024]{0:T(1024)S(1)} %bitcast.615, f32[1024]{0:T(1024)S(1)} %bitcast.608, f32[1024]{0:T(1024)S(1)} %bitcast.617, f32[1024]{0:T(1024)S(1)} %bitcast.604, ...), kind=kLoop, calls=%fused_computation.76.clone.1 | loop fusion | flops 72350720 | bytes 90112 | tf_op jit(solution)/shard_map/transpose(jvp())/while/body/eval_jaxpr/checkpoint/reduce_sum | solution.py:92
  88.7 15.9 %fusion.521 = (f32[1024]{0:T(1024)S(1)}, f32[1024]{0:T(1024)S(1)}, f32[1024]{0:T(1024)S(1)}, f32[1024]{0:T(1024)S(1)}, f32[1024]{0:T(1024)S(1)}, /*index=5*/f32[1024]{0:T(1024)S(1)}) fusion(f32[1024]{0:T(1024)S(1)} %bitcast.605, f32[1024]{0:T(1024)S(1)} %bitcast.614, f32[1024]{0:T(1024)S(1)} %bitcast.609, f32[1024]{0:T(1024)S(1)} %bitcast.618, ...), kind=kLoop, calls=%fused_computation.89.clone.1 | loop fusion | flops 88074240 | bytes 110592 | tf_op jit(solution)/shard_map/transpose(jvp())/while/body/eval_jaxpr/checkpoint/reduce_sum | solution.py:77
  105.2 14.4 %multiply_reduce_fusion.20 = f32[1024]{0:T(1024)S(1)} fusion(f32[1024]{0:T(1024)S(1)} %bitcast.599, f32[1024]{0:T(1024)S(1)} %get-tuple-element.2180, f32[1024]{0:T(1024)S(1)} %bitcast.606, f32[1024]{0:T(1024)S(1)} %bitcast.615, f32[1024]{0:T(1024)S(1)} %bitcast.608, f32[1024]{0:T(1024)S(1)} %bitcast.617, f32[1024]{0:T(1024)S(1)} %bitcast.604, ...), kind=kLoop, calls=%fused_computation.76.clone.1 | loop fusion | flops 72350720 | bytes 90112 | tf_op jit(solution)/shard_map/transpose(jvp())/while/body/eval_jaxpr/checkpoint/reduce_sum | solution.py:92
  119.6 15.9 %fusion.521 = (f32[1024]{0:T(1024)S(1)}, f32[1024]{0:T(1024)S(1)}, f32[1024]{0:T(1024)S(1)}, f32[1024]{0:T(1024)S(1)}, f32[1024]{0:T(1024)S(1)}, /*index=5*/f32[1024]{0:T(1024)S(1)}) fusion(f32[1024]{0:T(1024)S(1)} %bitcast.605, f32[1024]{0:T(1024)S(1)} %bitcast.614, f32[1024]{0:T(1024)S(1)} %bitcast.609, f32[1024]{0:T(1024)S(1)} %bitcast.618, ...), kind=kLoop, calls=%fused_computation.89.clone.1 | loop fusion | flops 88074240 | bytes 110592 | tf_op jit(solution)/shard_map/transpose(jvp())/while/body/eval_jaxpr/checkpoint/reduce_sum | solution.py:77
  138.8 3.7 %fusion.382 = (f32[2,4,128]{2,1,0:T(4,128)S(1)}, f32[2,4,128]{2,1,0:T(4,128)S(1)}, f32[2,4,128]{2,1,0:T(4,128)S(1)}, f32[2,4,128]{2,1,0:T(4,128)S(1)}, f32[2,4,1...) fusion(f32[2,4,128]{2,1,0:T(4,128)S(1)} %get-tuple-element.1743, ...), kind=kLoop, calls=%fused_computation.648 | loop fusion | flops 13352960 | bytes 126992 | tf_op jit(solution)/shard_map/transpose(jvp())/reduce_sum | solution.py:50
  142.7 3.7 %fusion.406 = (f32[2,4,128]{2,1,0:T(4,128)S(1)}, f32[2,4,128]{2,1,0:T(4,128)S(1)}, f32[2,4,128]{2,1,0:T(4,128)S(1)}, f32[2,4,128]{2,1,0:T(4,128)S(1)}, f32[2,4,1...) fusion(f32[2,4,128]{2,1,0:T(4,128)S(1)} %get-tuple-element.1739, ...), kind=kLoop, calls=%fused_computation.672 | loop fusion | flops 13352960 | bytes 126992 | tf_op jit(solution)/shard_map/transpose(jvp())/reduce_sum | solution.py:50
  146.6 3.7 %fusion.430 = (f32[2,4,128]{2,1,0:T(4,128)S(1)}, f32[2,4,128]{2,1,0:T(4,128)S(1)}, f32[2,4,128]{2,1,0:T(4,128)S(1)}, f32[2,4,128]{2,1,0:T(4,128)S(1)}, f32[2,4,1...) fusion(f32[2,4,128]{2,1,0:T(4,128)S(1)} %get-tuple-element.1759, ...), kind=kLoop, calls=%fused_computation.696 | loop fusion | flops 13352960 | bytes 126992 | tf_op jit(solution)/shard_map/transpose(jvp())/reduce_sum | solution.py:50
  150.5 5.0 %fusion.358 = (f32[2,4,128]{2,1,0:T(4,128)S(1)}, f32[2,4,128]{2,1,0:T(4,128)S(1)}, f32[2,4,128]{2,1,0:T(4,128)S(1)}, f32[2,4,128]{2,1,0:T(4,128)S(1)}, f32[2,4,1...) fusion(f32[2,4,128]{2,1,0:T(4,128)S(1)} %get-tuple-element.1734, ...), kind=kLoop, calls=%fused_computation.624 | loop fusion | flops 20029440 | bytes 180240 | tf_op jit(solution)/shard_map/transpose(jvp())/reduce_sum | solution.py:50
  164.6 2.1 collective-permute-done.11
  173.3 2.8 %fusion.360 = (f32[2,4,128]{2,1,0:T(4,128)S(1)}, f32[2,4,128]{2,1,0:T(4,128)S(1)}, f32[2,4,128]{2,1,0:T(4,128)S(1)}, f32[2,4,128]{2,1,0:T(4,128)S(1)}, f32[2,4,1...) fusion(f32[2,4,128]{2,1,0:T(4,128)S(1)} %get-tuple-element.1734, ...), kind=kLoop, calls=%fused_computation.626 | loop fusion | flops 11778048 | bytes 155664 | tf_op jit(solution)/shard_map/transpose(jvp())/reduce_sum | solution.py:50
  180.6 28.3 %while.64 = (s32[]{:T(128)}, f32[3,1024]{1,0:T(4,128)S(1)}, f32[1024]{0:T(1024)S(1)}, f32[2,3,1024]{2,1,0:T(4,128)S(1)}, f32[2,3,1024]{2,1,0:T(4,128)S(1)}, /*in...) while((s32[]{:T(128)}, f32[3,1024]{1,0:T(4,128)S(1)}, ...), condition=%wide.region_74.75_spmd.clone, body=%wide.region_67.74_spmd.clone.sunk | while | flops 78705664 | bytes 426451 | solution.py:115
  181.1 13.6 %fusion.524 = (f32[1024]{0:T(1024)S(1)}, f32[1024]{0:T(1024)S(1)}, f32[1024]{0:T(1024)S(1)}, f32[1024]{0:T(1024)S(1)}, f32[1024]{0:T(1024)S(1)}, /*index=5*/f32[1024]{0:T(1024)S(1)}) fusion(f32[1024]{0:T(1024)S(1)} %bitcast.610, f32[1024]{0:T(1024)S(1)} %bitcast.619, f32[1024]{0:T(1024)S(1)} %bitcast.612, f32[1024]{0:T(1024)S(1)} %bitcast.621, ...), kind=kLoop, calls=%fused_computation.178.clone.1 | loop fusion | flops 78637056 | bytes 106496 | tf_op jit(solution)/shard_map/transpose(jvp())/while/body/eval_jaxpr/checkpoint/reduce_sum | solution.py:77
  195.2 13.6 %fusion.524 = (f32[1024]{0:T(1024)S(1)}, f32[1024]{0:T(1024)S(1)}, f32[1024]{0:T(1024)S(1)}, f32[1024]{0:T(1024)S(1)}, f32[1024]{0:T(1024)S(1)}, /*index=5*/f32[1024]{0:T(1024)S(1)}) fusion(f32[1024]{0:T(1024)S(1)} %bitcast.610, f32[1024]{0:T(1024)S(1)} %bitcast.619, f32[1024]{0:T(1024)S(1)} %bitcast.612, f32[1024]{0:T(1024)S(1)} %bitcast.621, ...), kind=kLoop, calls=%fused_computation.178.clone.1 | loop fusion | flops 78637056 | bytes 106496 | tf_op jit(solution)/shard_map/transpose(jvp())/while/body/eval_jaxpr/checkpoint/reduce_sum | solution.py:77
  212.4 24.8 %reduce-scatter.7.cloned.1.call-done = f32[512,3]{1,0:T(8,128)} async-done(((f32[2048,3]{1,0:T(8,128)}), f32[512,3]{1,0:T(8,128)}) %reduce-scatter.7.cloned.1.call-update) | async-done | bytes 6160
  237.2 21.3 %reduce-scatter.9.cloned.1.call-done = f32[128,3]{1,0:T(8,128)} async-done(((f32[512,3]{1,0:T(8,128)}), f32[128,3]{1,0:T(8,128)}) %reduce-scatter.9.cloned.1.call-update) | async-done | bytes 1552
  (368 shorter events, 49.0 us)
Async XLA Ops:
  7.2 37.0 %copy-start = (f32[3,2,4,128]{3,2,1,0:T(4,128)S(1)}, f32[3,2,4,128]{3,2,1,0:T(4,128)}, u32[]{:S(2)}) copy-start(f32[3,2,4,128]{3,2,1,0:T(4,128)} %param.27) | copy-start | bytes 36868
  7.2 37.6 %copy-start.2 = (f32[2,4,128]{2,1,0:T(4,128)S(1)}, f32[2,4,128]{2,1,0:T(4,128)}, u32[]{:S(2)}) copy-start(f32[2,4,128]{2,1,0:T(4,128)} %param.29) | copy-start | bytes 12292
  7.2 37.6 %copy-start.3 = (f32[2,4,128]{2,1,0:T(4,128)S(1)}, f32[2,4,128]{2,1,0:T(4,128)}, u32[]{:S(2)}) copy-start(f32[2,4,128]{2,1,0:T(4,128)} %param.28) | copy-start | bytes 12292
  7.2 230.0 %reduce-scatter.7.cloned.1.call-start = ((), (), s32[]{:S(2)}) async-start(), calls=%async_computation.2 | async-start | bytes 1310720
  8.0 32.8 %collective-permute-start = (f32[5,1,4,128]{3,2,1,0:T(4,128)S(1)}, f32[5,1,4,128]{3,2,1,0:T(4,128)S(1)}, u32[]{:S(2)}, u32[]{:S(2)}) collective-permute-start(f32[5,1,4,128]{3,2,1,0:T(4,128)S(1)} %get-tuple-element.1764), channel_id=1, source_target_pairs={{0,4},{4,8},{8,12},{12,0},{1,5},{5,9},{9,13},{13,1},{2,6},{6,10},{... | collective-permute-start | bytes 30728 | tf_op jit(solution)/shard_map/ppermute | solution.py:26
  11.1 29.7 %collective-permute-start.1 = (f32[5,1,4,128]{3,2,1,0:T(4,128)S(1)}, f32[5,1,4,128]{3,2,1,0:T(4,128)S(1)}, u32[]{:S(2)}, u32[]{:S(2)}) collective-permute-start(f32[5,1,4,128]{3,2,1,0:T(4,128)S(1)} %get-tuple-element.1765), channel_id=1, source_target_pairs={{4,0},{8,4},{12,8},{0,12},{5,1},{9,5},{13,9},{1,13},{6,2},{10,6},{... | collective-permute-start | bytes 30728 | tf_op jit(solution)/shard_map/ppermute | solution.py:28
  41.6 3.1 %collective-permute-start.2 = (f32[5,4,1,128]{3,2,1,0:T(1,128)S(1)}, f32[5,4,1,128]{3,2,1,0:T(1,128)S(1)}, u32[]{:S(2)}, u32[]{:S(2)}) collective-permute-start(f32[5,4,1,128]{3,2,1,0:T(1,128)S(1)} %get-tuple-element.1746), channel_id=1, source_target_pairs={{0,1},{1,2},{2,3},{3,0},{4,5},{5,6},{6,7},{7,4},{8,9},{9,10},{10,1... | collective-permute-start | bytes 30728 | tf_op jit(solution)/shard_map/ppermute | solution.py:26
  41.7 24.1 %collective-permute-start.3 = (f32[5,4,1,128]{3,2,1,0:T(1,128)S(1)}, f32[5,4,1,128]{3,2,1,0:T(1,128)S(1)}, u32[]{:S(2)}, u32[]{:S(2)}) collective-permute-start(f32[5,4,1,128]{3,2,1,0:T(1,128)S(1)} %get-tuple-element.1747), channel_id=1, source_target_pairs={{1,0},{2,1},{3,2},{0,3},{5,4},{6,5},{7,6},{4,7},{9,8},{10,9},{11,1... | collective-permute-start | bytes 30728 | tf_op jit(solution)/shard_map/ppermute | solution.py:28
  44.9 28.9 %copy-start.1 = (s32[2,4,8]{2,1,0:T(4,128)S(1)}, s32[2,4,8]{2,1,0:T(4,128)}, u32[]{:S(2)}) copy-start(s32[2,4,8]{2,1,0:T(4,128)} %param.31) | copy-start | bytes 772
  69.9 65.8 %collective-permute-start.4 = (f32[1,4,128]{2,1,0:T(4,128)S(1)}, f32[1,4,128]{2,1,0:T(4,128)S(1)}, u32[]{:S(2)}, u32[]{:S(2)}) collective-permute-start(f32[1,4,128]{2,1,0:T(4,128)S(1)} %get-tuple-element.1813), channel_id=1, source_target_pairs={{0,4},{4,8},{8,12},{12,0},{1,5},{5,9},{9,13},{13,1},{2,6},{6,10},{... | collective-permute-start | bytes 6152 | tf_op jit(solution)/shard_map/ppermute | solution.py:26
  70.1 65.6 %collective-permute-start.5 = (f32[1,4,128]{2,1,0:T(4,128)S(1)}, f32[1,4,128]{2,1,0:T(4,128)S(1)}, u32[]{:S(2)}, u32[]{:S(2)}) collective-permute-start(f32[1,4,128]{2,1,0:T(4,128)S(1)} %get-tuple-element.1814), channel_id=1, source_target_pairs={{4,0},{8,4},{12,8},{0,12},{5,1},{9,5},{13,9},{1,13},{6,2},{10,6},{... | collective-permute-start | bytes 6152 | tf_op jit(solution)/shard_map/ppermute | solution.py:28
  135.6 31.0 %copy-start.4 = (f32[1024]{0:T(1024)}, f32[1024]{0:T(1024)S(1)}, u32[]{:S(2)}) copy-start(f32[1024]{0:T(1024)S(1)} %get-tuple-element.2483) | copy-start | bytes 12292
  135.7 3.1 %collective-permute-start.7 = (f32[4,1,128]{2,1,0:T(1,128)S(1)}, f32[4,1,128]{2,1,0:T(1,128)S(1)}, u32[]{:S(2)}, u32[]{:S(2)}) collective-permute-start(f32[4,1,128]{2,1,0:T(1,128)S(1)} %get-tuple-element.1809), channel_id=1, source_target_pairs={{0,1},{1,2},{2,3},{3,0},{4,5},{5,6},{6,7},{7,4},{8,9},{9,10},{10,1... | collective-permute-start | bytes 6152 | tf_op jit(solution)/shard_map/ppermute | solution.py:26
  135.8 3.0 %collective-permute-start.6 = (f32[4,1,128]{2,1,0:T(1,128)S(1)}, f32[4,1,128]{2,1,0:T(1,128)S(1)}, u32[]{:S(2)}, u32[]{:S(2)}) collective-permute-start(f32[4,1,128]{2,1,0:T(1,128)S(1)} %get-tuple-element.1810), channel_id=1, source_target_pairs={{1,0},{2,1},{3,2},{0,3},{5,4},{6,5},{7,6},{4,7},{9,8},{10,9},{11,1... | collective-permute-start | bytes 6152 | tf_op jit(solution)/shard_map/ppermute | solution.py:28
  155.8 3.1 %collective-permute-start.8 = (f32[1,4,128]{2,1,0:T(4,128)S(1)}, f32[1,4,128]{2,1,0:T(4,128)S(1)}, u32[]{:S(2)}, u32[]{:S(2)}) collective-permute-start(f32[1,4,128]{2,1,0:T(4,128)S(1)} %get-tuple-element.1794), channel_id=1, source_target_pairs={{0,3},{1,0},{2,1},{3,2},{4,7},{5,4},{6,5},{7,6},{8,11},{9,8},{10,9... | collective-permute-start | bytes 6152 | tf_op jit(solution)/shard_map/ppermute | solution.py:16
  157.8 3.1 %collective-permute-start.9 = (f32[1,4,128]{2,1,0:T(4,128)S(1)}, f32[1,4,128]{2,1,0:T(4,128)S(1)}, u32[]{:S(2)}, u32[]{:S(2)}) collective-permute-start(f32[1,4,128]{2,1,0:T(4,128)S(1)} %get-tuple-element.1793), channel_id=1, source_target_pairs={{0,1},{1,2},{2,3},{3,0},{4,5},{5,6},{6,7},{7,4},{8,9},{9,10},{10,1... | collective-permute-start | bytes 6152 | tf_op jit(solution)/shard_map/ppermute | solution.py:16
  160.9 3.6 %collective-permute-start.10 = (f32[1,4,128]{2,1,0:T(4,128)S(1)}, f32[1,4,128]{2,1,0:T(4,128)S(1)}, u32[]{:S(2)}, u32[]{:S(2)}) collective-permute-start(f32[1,4,128]{2,1,0:T(4,128)S(1)} %get-tuple-element.1808), channel_id=1, source_target_pairs={{0,12},{4,0},{8,4},{12,8},{1,13},{5,1},{9,5},{13,9},{2,14},{6,2},{... | collective-permute-start | bytes 6152 | tf_op jit(solution)/shard_map/ppermute | solution.py:16
  161.2 5.4 %collective-permute-start.11 = (f32[1,4,128]{2,1,0:T(4,128)S(1)}, f32[1,4,128]{2,1,0:T(4,128)S(1)}, u32[]{:S(2)}, u32[]{:S(2)}) collective-permute-start(f32[1,4,128]{2,1,0:T(4,128)S(1)} %get-tuple-element.1807), channel_id=1, source_target_pairs={{0,4},{4,8},{8,12},{12,0},{1,5},{5,9},{9,13},{13,1},{2,6},{6,10},{... | collective-permute-start | bytes 6152 | tf_op jit(solution)/shard_map/ppermute | solution.py:16
  177.0 1.4 collective-permute-start.12
  177.1 3.2 %collective-permute-start.13 = (f32[3,4,128]{2,0,1:T(4,128)S(1)}, f32[3,4,128]{2,0,1:T(4,128)S(1)}, u32[]{:S(2)}, u32[]{:S(2)}) collective-permute-start(f32[3,4,128]{2,0,1:T(4,128)S(1)} %get-tuple-element.1744), channel_id=1, source_target_pairs={{0,1},{1,2},{2,3},{3,0},{4,5},{5,6},{6,7},{7,4},{8,9},{9,10},{10,1... | collective-permute-start | bytes 18440 | tf_op jit(solution)/shard_map/ppermute | solution.py:16
  180.2 32.2 %collective-permute-start.14 = (f32[3,4,128]{2,0,1:T(4,128)S(1)}, f32[3,4,128]{2,0,1:T(4,128)S(1)}, u32[]{:S(2)}, u32[]{:S(2)}) collective-permute-start(f32[3,4,128]{2,0,1:T(4,128)S(1)} %get-tuple-element.1749), channel_id=1, source_target_pairs={{0,12},{4,0},{8,4},{12,8},{1,13},{5,1},{9,5},{13,9},{2,14},{6,2},{... | collective-permute-start | bytes 18440 | tf_op jit(solution)/shard_map/ppermute | solution.py:16
  210.3 49.2 %copy-start.5 = (s32[2,4,128]{2,1,0:T(4,128)S(1)}, s32[2,4,128]{2,1,0:T(4,128)}, u32[]{:S(2)}) copy-start(s32[2,4,128]{2,1,0:T(4,128)} %param.30) | copy-start | bytes 12292
  210.3 48.2 %reduce-scatter.9.cloned.1.call-start = ((), (), s32[]{:S(2)}) async-start(), calls=%async_computation.3 | async-start | bytes 327680
  210.4 26.8 %collective-permute-start.15 = (f32[3,4,128]{2,0,1:T(4,128)S(1)}, f32[3,4,128]{2,0,1:T(4,128)S(1)}, u32[]{:S(2)}, u32[]{:S(2)}) collective-permute-start(f32[3,4,128]{2,0,1:T(4,128)S(1)} %get-tuple-element.1748), channel_id=1, source_target_pairs={{0,4},{4,8},{8,12},{12,0},{1,5},{5,9},{9,13},{13,1},{2,6},{6,10},{... | collective-permute-start | bytes 18440 | tf_op jit(solution)/shard_map/ppermute | solution.py:16
Sparse Core Ops, SparseCore 0:
  210.4 26.7 reduce-scatter.6
  239.8 18.7 reduce-scatter.8
where the time goes:
time: 268 us; the launch traced here: 267 us
  other arithmetic  146 us (54%)
  waiting for transfers between devices  57.1 us (21%)
  starting transfers between devices  19.6 us (7%)
  blocking collectives  18.3 us (7%)
  between operations  15.6 us (6%)
  local copies, waits for them, and re-layouts  6.67 us (2%)
  matrix products  3.78 us (1%)
    reduce_sum x4, other arithmetic, centre_distance(): apart_axis = flat_pos[axis_slot][:, None] - centre[axis_slot][None, :]  59 us
    unnamed x4, waiting for transfers between devices  46.1 us
    reduce_sum x2, other arithmetic, potential_block(): product = flat_born[:, None] * comp_radius[None, :]  28.8 us
    reduce_sum x8, other arithmetic, pair_distance(): own_pos[axis_slot][..., :, None] - part_pos[axis_slot][..., None, :]  25.1 us
    reduce_sum x2, other arithmetic, screen_block(): jnp.sum(jnp.where(keep, volume * weight / (denom_sq * denom_sq), 0.0), ax...  19.9 us
    all_gather x1, blocking collectives, local(): all_table = lax.all_gather(sub_table, 'dom', axis=1, tiled=True)  13.1 us
    ppermute x4, starting transfers between devices, extended(): lax.ppermute(head, axis, [((i + 1) % count, i) for i in range(count)])  9.21 us
    ppermute x8, waiting for transfers between devices, passed_along(): lax.ppermute(shard, axis, [(i, (i + by) % size) for i in range(size)])  9.12 us
  transfers between devices with their start and end apart: 18, of which 10 were waited for; matrix products, arithmetic and copies ran while one was open for 46% of the time, Pallas kernels for 0%

commit v1 on v0

--- a/solution.py
+++ b/solution.py
@@ -201,7 +201,25 @@
         axis=0,
     )
     sub_table = lax.all_gather(comp_table, "sub", axis=1, tiled=True)
-    all_table = lax.all_gather(sub_table, "dom", axis=1, tiled=True)
+    count_2, index, rows = (lax.axis_size("dom"), lax.axis_index("dom"), sub_table.shape[1])
+    right = [(i_2, (i_2 + 1) % count_2) for i_2 in range(count_2)]
+    left = [(i_2, (i_2 - 1) % count_2) for i_2 in range(count_2)]
+    all_table = jnp.zeros(
+        (*sub_table.shape[:1], count_2 * rows, *sub_table.shape[1 + 1 :]), sub_table.dtype
+    )
+    all_table = lax.dynamic_update_slice_in_dim(all_table, sub_table, index * rows, axis=1)
+    from_left = from_right = sub_table
+    half = count_2 // 2
+    for step in range(1, half + 1):
+        from_left = lax.ppermute(from_left, "dom", right)
+        all_table = lax.dynamic_update_slice_in_dim(
+            all_table, from_left, (index - step) % count_2 * rows, axis=1
+        )
+        if step < count_2 - half:
+            from_right = lax.ppermute(from_right, "dom", left)
+            all_table = lax.dynamic_update_slice_in_dim(
+                all_table, from_right, (index + step) % count_2 * rows, axis=1
+            )
     all_centre = all_table[0:3]
     all_charge = all_table[3]
     all_volume = all_table[4]

time: 268 us -> 266 us (level)
  blocking collectives: 18.3 us -> 6.19 us
  starting transfers between devices: 19.6 us -> 24.7 us
  waiting for transfers between devices: 57.1 us -> 61.2 us
    all_gather x1 -> x0, blocking collectives: 13.1 us -> none  [local(): all_table = lax.all_gather(sub_table, 'dom', axis=1, tiled=True)]
    ppermute x0 -> x3, starting transfers between devices: none -> 4.11 us  [the longest x1 4.05 us: local(): from_right = lax.ppermute(from_right, 'dom', left)]
    ppermute x4, starting transfers between devices: 3.4 us -> 0.41 us  [extended(): lax.ppermute(tail, axis, [(i, (i + 1) % count) for i in range(count)])]
  transfers between devices with their start and end apart: 18 -> 21, of which waited for: 10 -> 11; matrix products, arithmetic and copies ran while one was open for 46% -> 39% of each run, Pallas kernels for 0% -> 0%
where the time goes in v1:
time: 266 us; the launch traced here: 265 us
  other arithmetic  146 us (55%)
  waiting for transfers between devices  61.2 us (23%)
  starting transfers between devices  24.7 us (9%)
  between operations  15.8 us (6%)
  local copies, waits for them, and re-layouts  6.7 us (3%)
  blocking collectives  6.19 us (2%)
  matrix products  3.78 us (1%)
    reduce_sum x4, other arithmetic, centre_distance(): apart_axis = flat_pos[axis_slot][:, None] - centre[axis_slot][None, :]  59 us
    unnamed x4, waiting for transfers between devices  46.1 us
    reduce_sum x2, other arithmetic, potential_block(): product = flat_born[:, None] * comp_radius[None, :]  28.8 us
    reduce_sum x8, other arithmetic, pair_distance(): own_pos[axis_slot][..., :, None] - part_pos[axis_slot][..., None, :]  25 us
    reduce_sum x2, other arithmetic, screen_block(): jnp.sum(jnp.where(keep, volume * weight / (denom_sq * denom_sq), 0.0), ax...  20 us
    ppermute x4, starting transfers between devices, extended(): lax.ppermute(head, axis, [((i + 1) % count, i) for i in range(count)])  11.4 us
    ppermute x8, waiting for transfers between devices, passed_along(): lax.ppermute(shard, axis, [(i, (i + by) % size) for i in range(size)])  11 us
    ppermute x8, starting transfers between devices, passed_along(): lax.ppermute(shard, axis, [(i, (i + by) % size) for i in range(size)])  8.68 us
  transfers between devices with their start and end apart: 21, of which 11 were waited for; matrix products, arithmetic and copies ran while one was open for 39% of the time, Pallas kernels for 0%

profile of v1, /device:TPU:0, one launch (start us, length us, event | category | flops | bytes accessed | tf_op | source)
XLA Modules:
  0.0 265.3 jit_solution(5730360558600535846)
XLA Ops:
  12.6 6.2 %all_gather.3 = f32[6,512]{1,0:T(8,128)S(1)} all-gather(f32[6,128]{1,0:T(8,128)S(1)} %pad_maximum_fusion.40), channel_id=1, replica_groups=mesh['groups'=2,'dom'=4,'sub'=4] {'sub'}, dimensions={1}, use_global_device_ids=true | all-gather | bytes 15360 | tf_op jit(solution)/shard_map/all_gather | solution.py:203
  18.8 4.0 %collective-permute-start.5 = (f32[6,512]{1,0:T(8,128)S(1)}, f32[6,512]{1,0:T(8,128)S(1)}, u32[]{:S(2)}, u32[]{:S(2)}) collective-permute-start(f32[6,512]{1,0:T(8,128)S(1)} %all_gather.3), channel_id=1, source_target_pairs={{0,12},{4,0},{8,4},{12,8},{1,13},{5,1},{9,5},{13,9},{2,14},{6,2},{... | collective-permute-start | bytes 36872 | tf_op jit(solution)/shard_map/ppermute | solution.py:219
  23.7 3.9 %collective-permute-start.1 = (f32[5,1,4,128]{3,2,1,0:T(4,128)S(1)}, f32[5,1,4,128]{3,2,1,0:T(4,128)S(1)}, u32[]{:S(2)}, u32[]{:S(2)}) collective-permute-start(f32[5,1,4,128]{3,2,1,0:T(4,128)S(1)} %get-tuple-element.1765), channel_id=1, source_target_pairs={{4,0},{8,4},{12,8},{0,12},{5,1},{9,5},{13,9},{1,13},{6,2},{10,6},{... | collective-permute-start | bytes 30728 | tf_op jit(solution)/shard_map/ppermute | solution.py:28
  41.3 21.0 %while.65 = (s32[]{:T(128)}, f32[1024]{0:T(1024)S(1)}, s32[2,1024]{1,0:T(2,128)S(1)}, s32[2,1024]{1,0:T(2,128)S(1)}, pred[1024,1]{0,1:T(4,128)(4,1)S(1)}, /*inde...) while((s32[]{:T(128)}, f32[1024]{0:T(1024)S(1)}, ...), condition=%wide.region_12.13_spmd.clone.clone.clone, body=%wide.region_10.12_spmd.clone.clone.clone.sunk | while | flops 50371588 | bytes 205115 | solution.py:115
  41.8 10.0 %select_reduce_fusion.11 = f32[1024]{0:T(1024)S(1)} fusion(f32[1024]{0:T(1024)S(1)} %bitcast.621, f32[1024]{0:T(1024)S(1)} %bitcast.591, f32[1024]{0:T(1024)S(1)} %bitcast.694, f32[1024]{0:T(1024)S(1)} %bitcast.590, f32[1024]{0:T(1024)S(1)} %bitcast.692, f32[1024]{0:T(1024)S(1)} %bitcast.589, f32[1024]{0:T(1024)S(1)} %bitcast.690, ...), kind=kLoop, calls=%fused_computation.229.clone.1 | loop fusion | flops 50330624 | bytes 81920 | tf_op jit(solution)/shard_map/jvp()/while/body/eval_jaxpr/reduce_sum | solution.py:86
  52.3 10.0 %select_reduce_fusion.11 = f32[1024]{0:T(1024)S(1)} fusion(f32[1024]{0:T(1024)S(1)} %bitcast.621, f32[1024]{0:T(1024)S(1)} %bitcast.591, f32[1024]{0:T(1024)S(1)} %bitcast.694, f32[1024]{0:T(1024)S(1)} %bitcast.590, f32[1024]{0:T(1024)S(1)} %bitcast.692, f32[1024]{0:T(1024)S(1)} %bitcast.589, f32[1024]{0:T(1024)S(1)} %bitcast.690, ...), kind=kLoop, calls=%fused_computation.229.clone.1 | loop fusion | flops 50330624 | bytes 81920 | tf_op jit(solution)/shard_map/jvp()/while/body/eval_jaxpr/reduce_sum | solution.py:86
  62.4 3.8 %collective-permute-start.8 = (f32[1,4,128]{2,1,0:T(4,128)S(1)}, f32[1,4,128]{2,1,0:T(4,128)S(1)}, u32[]{:S(2)}, u32[]{:S(2)}) collective-permute-start(f32[1,4,128]{2,1,0:T(4,128)S(1)} %get-tuple-element.1814), channel_id=1, source_target_pairs={{4,0},{8,4},{12,8},{0,12},{5,1},{9,5},{13,9},{1,13},{6,2},{10,6},{... | collective-permute-start | bytes 6152 | tf_op jit(solution)/shard_map/ppermute | solution.py:28
  68.1 61.9 %while.63 = (s32[]{:T(128)}, f32[3,1024]{1,0:T(4,128)S(1)}, f32[1024]{0:T(1024)S(1)}, f32[1024]{0:T(1024)S(1)}, f32[2,3,1024]{2,1,0:T(4,128)S(1)}, /*index=5*/f3...) while((s32[]{:T(128)}, f32[3,1024]{1,0:T(4,128)S(1)}, ...), condition=%wide.region_21.22_spmd.clone, body=%wide.region_13.21_spmd.clone.sunk | while | flops 160494592 | bytes 520676 | solution.py:139
  68.6 14.4 %multiply_reduce_fusion.20 = f32[1024]{0:T(1024)S(1)} fusion(f32[1024]{0:T(1024)S(1)} %bitcast.598, f32[1024]{0:T(1024)S(1)} %get-tuple-element.2180, f32[1024]{0:T(1024)S(1)} %bitcast.605, f32[1024]{0:T(1024)S(1)} %bitcast.614, f32[1024]{0:T(1024)S(1)} %bitcast.607, f32[1024]{0:T(1024)S(1)} %bitcast.616, f32[1024]{0:T(1024)S(1)} %bitcast.603, ...), kind=kLoop, calls=%fused_computation.76.clone.1 | loop fusion | flops 72350720 | bytes 90112 | tf_op jit(solution)/shard_map/transpose(jvp())/while/body/eval_jaxpr/checkpoint/reduce_sum | solution.py:92
  82.9 16.0 %fusion.518 = (f32[1024]{0:T(1024)S(1)}, f32[1024]{0:T(1024)S(1)}, f32[1024]{0:T(1024)S(1)}, f32[1024]{0:T(1024)S(1)}, f32[1024]{0:T(1024)S(1)}, /*index=5*/f32[1024]{0:T(1024)S(1)}) fusion(f32[1024]{0:T(1024)S(1)} %bitcast.604, f32[1024]{0:T(1024)S(1)} %bitcast.613, f32[1024]{0:T(1024)S(1)} %bitcast.608, f32[1024]{0:T(1024)S(1)} %bitcast.617, ...), kind=kLoop, calls=%fused_computation.89.clone.1 | loop fusion | flops 88074240 | bytes 110592 | tf_op jit(solution)/shard_map/transpose(jvp())/while/body/eval_jaxpr/checkpoint/reduce_sum | solution.py:77
  99.5 14.4 %multiply_reduce_fusion.20 = f32[1024]{0:T(1024)S(1)} fusion(f32[1024]{0:T(1024)S(1)} %bitcast.598, f32[1024]{0:T(1024)S(1)} %get-tuple-element.2180, f32[1024]{0:T(1024)S(1)} %bitcast.605, f32[1024]{0:T(1024)S(1)} %bitcast.614, f32[1024]{0:T(1024)S(1)} %bitcast.607, f32[1024]{0:T(1024)S(1)} %bitcast.616, f32[1024]{0:T(1024)S(1)} %bitcast.603, ...), kind=kLoop, calls=%fused_computation.76.clone.1 | loop fusion | flops 72350720 | bytes 90112 | tf_op jit(solution)/shard_map/transpose(jvp())/while/body/eval_jaxpr/checkpoint/reduce_sum | solution.py:92
  113.9 16.0 %fusion.518 = (f32[1024]{0:T(1024)S(1)}, f32[1024]{0:T(1024)S(1)}, f32[1024]{0:T(1024)S(1)}, f32[1024]{0:T(1024)S(1)}, f32[1024]{0:T(1024)S(1)}, /*index=5*/f32[1024]{0:T(1024)S(1)}) fusion(f32[1024]{0:T(1024)S(1)} %bitcast.604, f32[1024]{0:T(1024)S(1)} %bitcast.613, f32[1024]{0:T(1024)S(1)} %bitcast.608, f32[1024]{0:T(1024)S(1)} %bitcast.617, ...), kind=kLoop, calls=%fused_computation.89.clone.1 | loop fusion | flops 88074240 | bytes 110592 | tf_op jit(solution)/shard_map/transpose(jvp())/while/body/eval_jaxpr/checkpoint/reduce_sum | solution.py:77
  133.3 3.7 %fusion.382 = (f32[2,4,128]{2,1,0:T(4,128)S(1)}, f32[2,4,128]{2,1,0:T(4,128)S(1)}, f32[2,4,128]{2,1,0:T(4,128)S(1)}, f32[2,4,128]{2,1,0:T(4,128)S(1)}, f32[2,4,1...) fusion(f32[2,4,128]{2,1,0:T(4,128)S(1)} %get-tuple-element.1743, ...), kind=kLoop, calls=%fused_computation.648 | loop fusion | flops 13352960 | bytes 126992 | tf_op jit(solution)/shard_map/transpose(jvp())/reduce_sum | solution.py:50
  137.2 3.7 %fusion.406 = (f32[2,4,128]{2,1,0:T(4,128)S(1)}, f32[2,4,128]{2,1,0:T(4,128)S(1)}, f32[2,4,128]{2,1,0:T(4,128)S(1)}, f32[2,4,128]{2,1,0:T(4,128)S(1)}, f32[2,4,1...) fusion(f32[2,4,128]{2,1,0:T(4,128)S(1)} %get-tuple-element.1739, ...), kind=kLoop, calls=%fused_computation.672 | loop fusion | flops 13352960 | bytes 126992 | tf_op jit(solution)/shard_map/transpose(jvp())/reduce_sum | solution.py:50
  141.1 3.7 %fusion.430 = (f32[2,4,128]{2,1,0:T(4,128)S(1)}, f32[2,4,128]{2,1,0:T(4,128)S(1)}, f32[2,4,128]{2,1,0:T(4,128)S(1)}, f32[2,4,128]{2,1,0:T(4,128)S(1)}, f32[2,4,1...) fusion(f32[2,4,128]{2,1,0:T(4,128)S(1)} %get-tuple-element.1759, ...), kind=kLoop, calls=%fused_computation.696 | loop fusion | flops 13352960 | bytes 126992 | tf_op jit(solution)/shard_map/transpose(jvp())/reduce_sum | solution.py:50
  145.0 5.0 %fusion.358 = (f32[2,4,128]{2,1,0:T(4,128)S(1)}, f32[2,4,128]{2,1,0:T(4,128)S(1)}, f32[2,4,128]{2,1,0:T(4,128)S(1)}, f32[2,4,128]{2,1,0:T(4,128)S(1)}, f32[2,4,1...) fusion(f32[2,4,128]{2,1,0:T(4,128)S(1)} %get-tuple-element.1734, ...), kind=kLoop, calls=%fused_computation.624 | loop fusion | flops 20029440 | bytes 180240 | tf_op jit(solution)/shard_map/transpose(jvp())/reduce_sum | solution.py:50
  155.4 3.9 %collective-permute-start.13 = (f32[1,4,128]{2,1,0:T(4,128)S(1)}, f32[1,4,128]{2,1,0:T(4,128)S(1)}, u32[]{:S(2)}, u32[]{:S(2)}) collective-permute-start(f32[1,4,128]{2,1,0:T(4,128)S(1)} %get-tuple-element.1808), channel_id=1, source_target_pairs={{0,12},{4,0},{8,4},{12,8},{1,13},{5,1},{9,5},{13,9},{2,14},{6,2},{... | collective-permute-start | bytes 6152 | tf_op jit(solution)/shard_map/ppermute | solution.py:16
  160.6 4.1 %collective-permute-done.14 = f32[1,4,128]{2,1,0:T(4,128)S(1)} collective-permute-done((f32[1,4,128]{2,1,0:T(4,128)S(1)}, f32[1,4,128]{2,1,0:T(4,128)S(1)}, u32[]{:S(2)}, u32[]{:S(2)}) %collective-permute-start.14) | collective-permute-done | bytes 2080 | tf_op jit(solution)/shard_map/ppermute | solution.py:16
  171.4 2.8 %fusion.360 = (f32[2,4,128]{2,1,0:T(4,128)S(1)}, f32[2,4,128]{2,1,0:T(4,128)S(1)}, f32[2,4,128]{2,1,0:T(4,128)S(1)}, f32[2,4,128]{2,1,0:T(4,128)S(1)}, f32[2,4,1...) fusion(f32[2,4,128]{2,1,0:T(4,128)S(1)} %get-tuple-element.1734, ...), kind=kLoop, calls=%fused_computation.626 | loop fusion | flops 11778048 | bytes 155664 | tf_op jit(solution)/shard_map/transpose(jvp())/reduce_sum | solution.py:50
  178.6 28.3 %while.64 = (s32[]{:T(128)}, f32[3,1024]{1,0:T(4,128)S(1)}, f32[1024]{0:T(1024)S(1)}, f32[2,3,1024]{2,1,0:T(4,128)S(1)}, f32[2,3,1024]{2,1,0:T(4,128)S(1)}, /*in...) while((s32[]{:T(128)}, f32[3,1024]{1,0:T(4,128)S(1)}, ...), condition=%wide.region_74.75_spmd.clone, body=%wide.region_67.74_spmd.clone.sunk | while | flops 78705664 | bytes 426451 | solution.py:115
  179.1 13.6 %fusion.521 = (f32[1024]{0:T(1024)S(1)}, f32[1024]{0:T(1024)S(1)}, f32[1024]{0:T(1024)S(1)}, f32[1024]{0:T(1024)S(1)}, f32[1024]{0:T(1024)S(1)}, /*index=5*/f32[1024]{0:T(1024)S(1)}) fusion(f32[1024]{0:T(1024)S(1)} %bitcast.609, f32[1024]{0:T(1024)S(1)} %bitcast.618, f32[1024]{0:T(1024)S(1)} %bitcast.611, f32[1024]{0:T(1024)S(1)} %bitcast.620, ...), kind=kLoop, calls=%fused_computation.178.clone.1 | loop fusion | flops 78637056 | bytes 106496 | tf_op jit(solution)/shard_map/transpose(jvp())/while/body/eval_jaxpr/checkpoint/reduce_sum | solution.py:77
  193.3 13.6 %fusion.521 = (f32[1024]{0:T(1024)S(1)}, f32[1024]{0:T(1024)S(1)}, f32[1024]{0:T(1024)S(1)}, f32[1024]{0:T(1024)S(1)}, f32[1024]{0:T(1024)S(1)}, /*index=5*/f32[1024]{0:T(1024)S(1)}) fusion(f32[1024]{0:T(1024)S(1)} %bitcast.609, f32[1024]{0:T(1024)S(1)} %bitcast.618, f32[1024]{0:T(1024)S(1)} %bitcast.611, f32[1024]{0:T(1024)S(1)} %bitcast.620, ...), kind=kLoop, calls=%fused_computation.178.clone.1 | loop fusion | flops 78637056 | bytes 106496 | tf_op jit(solution)/shard_map/transpose(jvp())/while/body/eval_jaxpr/checkpoint/reduce_sum | solution.py:77
  210.5 24.8 %reduce-scatter.7.cloned.1.call-done = f32[512,3]{1,0:T(8,128)} async-done(((f32[2048,3]{1,0:T(8,128)}), f32[512,3]{1,0:T(8,128)}) %reduce-scatter.7.cloned.1.call-update) | async-done | bytes 6160
  235.3 21.3 %reduce-scatter.9.cloned.1.call-done = f32[128,3]{1,0:T(8,128)} async-done(((f32[512,3]{1,0:T(8,128)}), f32[128,3]{1,0:T(8,128)}) %reduce-scatter.9.cloned.1.call-update) | async-done | bytes 1552
  (378 shorter events, 50.1 us)
Async XLA Ops:
  7.2 28.5 %copy-start.2 = (f32[2,4,128]{2,1,0:T(4,128)S(1)}, f32[2,4,128]{2,1,0:T(4,128)}, u32[]{:S(2)}) copy-start(f32[2,4,128]{2,1,0:T(4,128)} %param.29) | copy-start | bytes 12292
  7.2 228.0 %reduce-scatter.7.cloned.1.call-start = ((), (), s32[]{:S(2)}) async-start(), calls=%async_computation.2 | async-start | bytes 1310720
  18.8 16.8 %collective-permute-start.5 = (f32[6,512]{1,0:T(8,128)S(1)}, f32[6,512]{1,0:T(8,128)S(1)}, u32[]{:S(2)}, u32[]{:S(2)}) collective-permute-start(f32[6,512]{1,0:T(8,128)S(1)} %all_gather.3), channel_id=1, source_target_pairs={{0,12},{4,0},{8,4},{12,8},{1,13},{5,1},{9,5},{13,9},{2,14},{6,2},{... | collective-permute-start | bytes 36872 | tf_op jit(solution)/shard_map/ppermute | solution.py:219
  22.9 12.7 %collective-permute-start.4 = (f32[6,512]{1,0:T(8,128)S(1)}, f32[6,512]{1,0:T(8,128)S(1)}, u32[]{:S(2)}, u32[]{:S(2)}) collective-permute-start(f32[6,512]{1,0:T(8,128)S(1)} %all_gather.3), channel_id=1, source_target_pairs={{0,4},{4,8},{8,12},{12,0},{1,5},{5,9},{9,13},{13,1},{2,6},{6,10},{... | collective-permute-start | bytes 36872 | tf_op jit(solution)/shard_map/ppermute | solution.py:214
  23.6 7.9 %collective-permute-start = (f32[5,1,4,128]{3,2,1,0:T(4,128)S(1)}, f32[5,1,4,128]{3,2,1,0:T(4,128)S(1)}, u32[]{:S(2)}, u32[]{:S(2)}) collective-permute-start(f32[5,1,4,128]{3,2,1,0:T(4,128)S(1)} %get-tuple-element.1764), channel_id=1, source_target_pairs={{0,4},{4,8},{8,12},{12,0},{1,5},{5,9},{9,13},{13,1},{2,6},{6,10},{... | collective-permute-start | bytes 30728 | tf_op jit(solution)/shard_map/ppermute | solution.py:26
  23.7 7.8 %collective-permute-start.1 = (f32[5,1,4,128]{3,2,1,0:T(4,128)S(1)}, f32[5,1,4,128]{3,2,1,0:T(4,128)S(1)}, u32[]{:S(2)}, u32[]{:S(2)}) collective-permute-start(f32[5,1,4,128]{3,2,1,0:T(4,128)S(1)} %get-tuple-element.1765), channel_id=1, source_target_pairs={{4,0},{8,4},{12,8},{0,12},{5,1},{9,5},{13,9},{1,13},{6,2},{10,6},{... | collective-permute-start | bytes 30728 | tf_op jit(solution)/shard_map/ppermute | solution.py:28
  32.3 3.4 %collective-permute-start.2 = (f32[5,4,1,128]{3,2,1,0:T(1,128)S(1)}, f32[5,4,1,128]{3,2,1,0:T(1,128)S(1)}, u32[]{:S(2)}, u32[]{:S(2)}) collective-permute-start(f32[5,4,1,128]{3,2,1,0:T(1,128)S(1)} %get-tuple-element.1746), channel_id=1, source_target_pairs={{0,1},{1,2},{2,3},{3,0},{4,5},{5,6},{6,7},{7,4},{8,9},{9,10},{10,1... | collective-permute-start | bytes 30728 | tf_op jit(solution)/shard_map/ppermute | solution.py:26
  32.4 3.3 %collective-permute-start.3 = (f32[5,4,1,128]{3,2,1,0:T(1,128)S(1)}, f32[5,4,1,128]{3,2,1,0:T(1,128)S(1)}, u32[]{:S(2)}, u32[]{:S(2)}) collective-permute-start(f32[5,4,1,128]{3,2,1,0:T(1,128)S(1)} %get-tuple-element.1747), channel_id=1, source_target_pairs={{1,0},{2,1},{3,2},{0,3},{5,4},{6,5},{7,6},{4,7},{9,8},{10,9},{11,1... | collective-permute-start | bytes 30728 | tf_op jit(solution)/shard_map/ppermute | solution.py:28
  35.6 5.6 %collective-permute-start.6 = (f32[6,512]{1,0:T(8,128)S(1)}, f32[6,512]{1,0:T(8,128)S(1)}, u32[]{:S(2)}, u32[]{:S(2)}) collective-permute-start(f32[6,512]{1,0:T(8,128)S(1)} %collective-permute-done.4), channel_id=1, source_target_pairs={{0,4},{4,8},{8,12},{12,0},{1,5},{5,9},{9,13},{13,1},{2,6},{6,10},{... | collective-permute-start | bytes 36872 | tf_op jit(solution)/shard_map/ppermute | solution.py:214
  62.4 5.4 %collective-permute-start.7 = (f32[1,4,128]{2,1,0:T(4,128)S(1)}, f32[1,4,128]{2,1,0:T(4,128)S(1)}, u32[]{:S(2)}, u32[]{:S(2)}) collective-permute-start(f32[1,4,128]{2,1,0:T(4,128)S(1)} %get-tuple-element.1813), channel_id=1, source_target_pairs={{0,4},{4,8},{8,12},{12,0},{1,5},{5,9},{9,13},{13,1},{2,6},{6,10},{... | collective-permute-start | bytes 6152 | tf_op jit(solution)/shard_map/ppermute | solution.py:26
  62.4 5.4 %collective-permute-start.8 = (f32[1,4,128]{2,1,0:T(4,128)S(1)}, f32[1,4,128]{2,1,0:T(4,128)S(1)}, u32[]{:S(2)}, u32[]{:S(2)}) collective-permute-start(f32[1,4,128]{2,1,0:T(4,128)S(1)} %get-tuple-element.1814), channel_id=1, source_target_pairs={{4,0},{8,4},{12,8},{0,12},{5,1},{9,5},{13,9},{1,13},{6,2},{10,6},{... | collective-permute-start | bytes 6152 | tf_op jit(solution)/shard_map/ppermute | solution.py:28
  67.8 64.1 %collective-permute-start.10 = (f32[4,1,128]{2,1,0:T(1,128)S(1)}, f32[4,1,128]{2,1,0:T(1,128)S(1)}, u32[]{:S(2)}, u32[]{:S(2)}) collective-permute-start(f32[4,1,128]{2,1,0:T(1,128)S(1)} %get-tuple-element.1809), channel_id=1, source_target_pairs={{0,1},{1,2},{2,3},{3,0},{4,5},{5,6},{6,7},{7,4},{8,9},{9,10},{10,1... | collective-permute-start | bytes 6152 | tf_op jit(solution)/shard_map/ppermute | solution.py:26
  129.9 34.8 %copy-start.4 = (f32[1024]{0:T(1024)}, f32[1024]{0:T(1024)S(1)}, u32[]{:S(2)}) copy-start(f32[1024]{0:T(1024)S(1)} %get-tuple-element.2483) | copy-start | bytes 12292
  130.0 3.3 %collective-permute-start.9 = (f32[4,1,128]{2,1,0:T(1,128)S(1)}, f32[4,1,128]{2,1,0:T(1,128)S(1)}, u32[]{:S(2)}, u32[]{:S(2)}) collective-permute-start(f32[4,1,128]{2,1,0:T(1,128)S(1)} %get-tuple-element.1810), channel_id=1, source_target_pairs={{1,0},{2,1},{3,2},{0,3},{5,4},{6,5},{7,6},{4,7},{9,8},{10,9},{11,1... | collective-permute-start | bytes 6152 | tf_op jit(solution)/shard_map/ppermute | solution.py:28
  150.3 3.1 %collective-permute-start.11 = (f32[1,4,128]{2,1,0:T(4,128)S(1)}, f32[1,4,128]{2,1,0:T(4,128)S(1)}, u32[]{:S(2)}, u32[]{:S(2)}) collective-permute-start(f32[1,4,128]{2,1,0:T(4,128)S(1)} %get-tuple-element.1794), channel_id=1, source_target_pairs={{0,3},{1,0},{2,1},{3,2},{4,7},{5,4},{6,5},{7,6},{8,11},{9,8},{10,9... | collective-permute-start | bytes 6152 | tf_op jit(solution)/shard_map/ppermute | solution.py:16
  152.3 3.1 %collective-permute-start.12 = (f32[1,4,128]{2,1,0:T(4,128)S(1)}, f32[1,4,128]{2,1,0:T(4,128)S(1)}, u32[]{:S(2)}, u32[]{:S(2)}) collective-permute-start(f32[1,4,128]{2,1,0:T(4,128)S(1)} %get-tuple-element.1793), channel_id=1, source_target_pairs={{0,1},{1,2},{2,3},{3,0},{4,5},{5,6},{6,7},{7,4},{8,9},{9,10},{10,1... | collective-permute-start | bytes 6152 | tf_op jit(solution)/shard_map/ppermute | solution.py:16
  155.4 5.2 %collective-permute-start.13 = (f32[1,4,128]{2,1,0:T(4,128)S(1)}, f32[1,4,128]{2,1,0:T(4,128)S(1)}, u32[]{:S(2)}, u32[]{:S(2)}) collective-permute-start(f32[1,4,128]{2,1,0:T(4,128)S(1)} %get-tuple-element.1808), channel_id=1, source_target_pairs={{0,12},{4,0},{8,4},{12,8},{1,13},{5,1},{9,5},{13,9},{2,14},{6,2},{... | collective-permute-start | bytes 6152 | tf_op jit(solution)/shard_map/ppermute | solution.py:16
  159.3 5.4 %collective-permute-start.14 = (f32[1,4,128]{2,1,0:T(4,128)S(1)}, f32[1,4,128]{2,1,0:T(4,128)S(1)}, u32[]{:S(2)}, u32[]{:S(2)}) collective-permute-start(f32[1,4,128]{2,1,0:T(4,128)S(1)} %get-tuple-element.1807), channel_id=1, source_target_pairs={{0,4},{4,8},{8,12},{12,0},{1,5},{5,9},{9,13},{13,1},{2,6},{6,10},{... | collective-permute-start | bytes 6152 | tf_op jit(solution)/shard_map/ppermute | solution.py:16
  175.0 1.4 collective-permute-start.15
  175.1 3.2 %collective-permute-start.16 = (f32[3,4,128]{2,0,1:T(4,128)S(1)}, f32[3,4,128]{2,0,1:T(4,128)S(1)}, u32[]{:S(2)}, u32[]{:S(2)}) collective-permute-start(f32[3,4,128]{2,0,1:T(4,128)S(1)} %get-tuple-element.1744), channel_id=1, source_target_pairs={{0,1},{1,2},{2,3},{3,0},{4,5},{5,6},{6,7},{7,4},{8,9},{9,10},{10,1... | collective-permute-start | bytes 18440 | tf_op jit(solution)/shard_map/ppermute | solution.py:16
  178.3 32.2 %collective-permute-start.17 = (f32[3,4,128]{2,0,1:T(4,128)S(1)}, f32[3,4,128]{2,0,1:T(4,128)S(1)}, u32[]{:S(2)}, u32[]{:S(2)}) collective-permute-start(f32[3,4,128]{2,0,1:T(4,128)S(1)} %get-tuple-element.1749), channel_id=1, source_target_pairs={{0,12},{4,0},{8,4},{12,8},{1,13},{5,1},{9,5},{13,9},{2,14},{6,2},{... | collective-permute-start | bytes 18440 | tf_op jit(solution)/shard_map/ppermute | solution.py:16
  208.3 49.2 %copy-start.5 = (s32[2,4,128]{2,1,0:T(4,128)S(1)}, s32[2,4,128]{2,1,0:T(4,128)}, u32[]{:S(2)}) copy-start(s32[2,4,128]{2,1,0:T(4,128)} %param.30) | copy-start | bytes 12292
  208.4 48.2 %reduce-scatter.9.cloned.1.call-start = ((), (), s32[]{:S(2)}) async-start(), calls=%async_computation.3 | async-start | bytes 327680
  208.4 26.8 %collective-permute-start.18 = (f32[3,4,128]{2,0,1:T(4,128)S(1)}, f32[3,4,128]{2,0,1:T(4,128)S(1)}, u32[]{:S(2)}, u32[]{:S(2)}) collective-permute-start(f32[3,4,128]{2,0,1:T(4,128)S(1)} %get-tuple-element.1748), channel_id=1, source_target_pairs={{0,4},{4,8},{8,12},{12,0},{1,5},{5,9},{9,13},{13,1},{2,6},{6,10},{... | collective-permute-start | bytes 18440 | tf_op jit(solution)/shard_map/ppermute | solution.py:16
  (3 other events, 83.9 us)
Sparse Core Ops, SparseCore 0:
  208.5 26.7 reduce-scatter.6
  237.8 18.7 reduce-scatter.8
